TPU v7x, 256 devices: a whole 4x4x8 slice. The times are simulated.
256 devices in a mesh: gx: 32 (over x, z_hi, core), sec: 8 (over z_lo, y).
Axes of the slice: x: 4, y: 4, z: 8 (z_hi: 4, z_lo: 2; z = z_hi * 2 + z_lo), core: 2. Of those that a mesh axis runs over, the one named last changes fastest.
Arguments:
- state_init: float32 [16, 256, 64, 128], P(None, 'gx', 'sec'), may hold values from -6 to 6
- rock_type: int32 [256, 4096], P('gx', 'sec'), may hold values from 0 to 15
- perm_table: float32 [3, 16], replicated, may hold values from 0.2 to 1
- well_cells: int32 [256], replicated, may hold values from 0 to 1048575
- well_rate: float32 [16, 256], replicated, may hold values from -12 to 12
- basis_in: bfloat16 [256, 64, 128, 256], P(('gx', 'sec')), may hold values from -4 to 4
- singular: float32 [256], replicated, may hold values from 0.5 to 2
Outputs:
- state_out: float32 [16, 256, 64, 128], P(None, 'gx', 'sec')
- basis_out: bfloat16 [256, 64, 128, 256], P(('gx', 'sec'))
- singular_out: float32 [256], replicated
All inputs are finite; a program needn't handle non-finite values.
Results may differ from a plain program's by a relative error of at most 0.0059.
Values may be sent and summed in bfloat16 or wider, within the bound.
A program may use at most 128 MiB of HBM per device.

v0:
```python
import jax
import jax.numpy as jnp
from jax import lax
from jax.sharding import PartitionSpec as P

MG = 8
STEPS = 4
GROUPS = 2
DT_PRESSURE = 0.12
DT_SATURATION = 0.06
DT_ADVECT = 0.15


def with_halo(block, sides, width):
    for axis, dim in sides:
        count = lax.axis_size(axis)
        forward = [(i, i + 1) for i in range(count - 1)]
        backward = [(target, source) for source, target in forward]
        low = lax.ppermute(
            lax.slice_in_dim(block, block.shape[dim] - width, None, axis=dim), axis, forward
        )
        high = lax.ppermute(lax.slice_in_dim(block, 0, width, axis=dim), axis, backward)
        block = jnp.concatenate([low, block, high], axis=dim)
    return block


def harmonic(left, right):
    return 2.0 * left * right / (left + right)


def shift_layers(fields):
    blank = jnp.zeros_like(fields[..., :1])
    return (
        jnp.concatenate([fields[..., 1:], blank], -1),
        jnp.concatenate([blank, fields[..., :-1]], -1),
    )


def advance(fields, besides, weights, inflow, layers):
    column = lax.broadcasted_iota(jnp.int32, (fields.shape[-1],), 0)
    step_sizes = jnp.where(column < layers, DT_PRESSURE, DT_SATURATION)
    is_sat = (column >= layers).astype(fields.dtype)
    press_both = jnp.concatenate([fields[..., :layers], fields[..., :layers]], -1)
    spread = jnp.zeros_like(fields)
    carried = jnp.zeros_like(fields)
    for beside, weight in zip(besides, weights):
        spread = spread + weight * (beside - fields)
        beside_press = jnp.concatenate([beside[..., :layers], beside[..., :layers]], -1)
        pushed = weight * (beside_press - press_both)
        carried = carried + jnp.maximum(pushed, 0.0) * beside + jnp.minimum(pushed, 0.0) * fields
    return fields + step_sizes * spread + DT_ADVECT * is_sat * carried + DT_PRESSURE * inflow


HIGH = lax.Precision.HIGHEST


def hdot(a, b):
    return jnp.dot(a, b, precision=HIGH)


def batch_update(coeffs, gram_of, sigma):
    rounded = coeffs.astype(jnp.bfloat16).astype(jnp.float32)
    gram = gram_of(coeffs, rounded)
    square = jnp.diag(sigma * sigma)
    total = square + hdot(coeffs.T, coeffs)
    inner = hdot(total, total) + hdot(coeffs.T, hdot(gram, coeffs))
    factor = jnp.linalg.cholesky(inner)
    eye = jnp.eye(sigma.shape[0], dtype=jnp.float32)
    back = lax.linalg.triangular_solve(factor, eye, left_side=True, lower=True).T
    top = sigma[:, None] * hdot(total, back)
    bottom = hdot(hdot(coeffs, total) + hdot(gram, coeffs), back)
    sigma_next = jnp.sqrt(jnp.sum(top * top, axis=0) + jnp.sum(bottom * bottom, axis=0))
    on_basis = hdot(square + hdot((coeffs - rounded).T, coeffs), back)
    on_snaps = hdot(coeffs, back)
    return (on_basis, on_snaps, sigma_next)


def small_algebra(uu, su, ss, sigma):
    half = su.shape[0] // 2
    s00, s10, s11 = (ss[:half, :half], ss[half:, :half], ss[half:, half:])

    def gram_first(c, r):
        cr = hdot(c, r.T)
        return s00 - cr - cr.T + hdot(r, hdot(uu, r.T))

    wu, ws, sigma1 = batch_update(su[:half], gram_first, sigma)
    coeffs1 = hdot(su[half:], wu) + hdot(s10, ws)

    def gram_second(c, r):
        cr = hdot(c, r.T)
        yu, ys = (hdot(wu, r.T), hdot(ws, r.T))
        mixed = hdot(ys.T, hdot(su[:half], yu))
        own = hdot(yu.T, hdot(uu, yu)) + mixed + mixed.T + hdot(ys.T, hdot(s00, ys))
        return s11 - cr - cr.T + own

    wu1, ws1, sigma2 = batch_update(coeffs1, gram_second, sigma1)
    return (hdot(wu, wu1), hdot(ws, wu1), ws1, sigma2)


def body(state_init, rock_type, perm_table, well_cells, well_rate, basis_in, singular):
    across = state_init.shape[1]
    along = state_init.shape[2]
    layers = state_init.shape[3] // 2
    sec_count = lax.axis_size("sec")
    rock_count = perm_table.shape[1]
    kinds = lax.broadcasted_iota(jnp.int32, (rock_count, 1, 1), 0)
    picks = (rock_type[None] == kinds).astype(jnp.float32)
    perm = jnp.einsum("dr,rxc->dxc", perm_table, picks, precision=lax.Precision.HIGHEST).reshape(
        3, across, along, layers
    )
    paired = jnp.concatenate([perm[0], perm[1]], -1)
    bordered_perm = with_halo(paired.astype(jnp.bfloat16), (("gx", 0), ("sec", 1)), 1).astype(
        paired.dtype
    )
    perm_xh = bordered_perm[..., :layers]
    perm_yh = bordered_perm[..., layers:]
    x_up = harmonic(perm[0], perm_xh[2:, 1:-1])
    x_down = harmonic(perm_xh[:-2, 1:-1], perm[0])
    y_up = harmonic(perm[1], perm_yh[1:-1, 2:])
    y_down = harmonic(perm_yh[1:-1, :-2], perm[1])
    z_padded = jnp.pad(perm[2], ((0, 0), (0, 0), (1, 1)))
    z_up = harmonic(perm[2], z_padded[..., 2:])
    z_down = harmonic(z_padded[..., :-2], perm[2])
    weights = [
        jnp.concatenate([face, face], -1) for face in (x_up, x_down, y_up, y_down, z_up, z_down)
    ]
    x_start = lax.axis_index("gx") * across
    y_start = lax.axis_index("sec") * along
    total_y = along * sec_count
    x_pos = lax.broadcasted_iota(jnp.int32, (across, along, layers), 0)
    y_pos = lax.broadcasted_iota(jnp.int32, (across, along, layers), 1)
    z_pos = lax.broadcasted_iota(jnp.int32, (across, along, layers), 2)
    cell_ids = ((x_start + x_pos) * total_y + y_start + y_pos) * layers + z_pos
    hits = (well_cells[:, None] == cell_ids.reshape(1, -1)).astype(jnp.float32)
    source = jnp.dot(well_rate, hits, precision=lax.Precision.HIGHEST).reshape(
        state_init.shape[0], across, along, layers
    )
    source_full = jnp.concatenate([source, jnp.zeros_like(source)], -1)
    local_rows = basis_in.shape[0] * basis_in.shape[1] * basis_in.shape[2]
    rows_total = local_rows * lax.axis_size("gx") * sec_count
    finals = []
    snaps = []
    for group in range(GROUPS):
        fields = state_init[group * MG : (group + 1) * MG]
        inflow = source_full[group * MG : (group + 1) * MG]
        saved = []
        for step_index in range(STEPS):
            bordered = with_halo(fields.astype(jnp.bfloat16), (("gx", 1), ("sec", 2)), 1).astype(
                fields.dtype
            )
            up_layer, down_layer = shift_layers(fields)
            besides = [
                bordered[:, 2:, 1:-1],
                bordered[:, :-2, 1:-1],
                bordered[:, 1:-1, 2:],
                bordered[:, 1:-1, :-2],
                up_layer,
                down_layer,
            ]
            fields = advance(fields, besides, weights, inflow, layers)
            snapshot = fields.astype(jnp.bfloat16)
            saved.append(snapshot)
        finals.append(fields)
        stacked = jnp.concatenate(saved, 0)
        stacked = lax.all_to_all(stacked, "sec", split_axis=1, concat_axis=2, tiled=True)
        snaps.append(stacked.reshape(stacked.shape[0], -1))
    both = jnp.concatenate(snaps, 0)
    basis = basis_in.reshape(both.shape[1], basis_in.shape[-1])
    count = basis.shape[1]
    uu = lax.dot_general(basis, basis, (((0,), (0,)), ((), ())), preferred_element_type=jnp.float32)
    su = jnp.dot(both, basis, preferred_element_type=jnp.float32)
    ss = lax.dot_general(both, both, (((1,), (1,)), ((), ())), preferred_element_type=jnp.float32)
    local = jnp.concatenate(
        [
            jnp.concatenate([uu, su], 0),
            jnp.pad(
                jnp.concatenate([jnp.zeros((count, both.shape[0]), jnp.float32), ss], 0),
                ((0, 0), (0, 64)),
            ),
        ],
        1,
    )
    whole = lax.psum(local, ("gx", "sec")) / rows_total
    w0, w1, w2, sigma = small_algebra(
        whole[:count, :count],
        whole[count:, :count],
        whole[count:, count : count + both.shape[0]],
        singular,
    )
    fresh = jnp.dot(basis, w0.astype(jnp.bfloat16), preferred_element_type=jnp.float32)
    fresh = fresh + lax.dot_general(
        both,
        jnp.concatenate([w1, w2], 0).astype(jnp.bfloat16),
        (((0,), (0,)), ((), ())),
        preferred_element_type=jnp.float32,
    )
    basis_now = fresh.astype(jnp.bfloat16).reshape(basis_in.shape)
    return (jnp.concatenate(finals, 0), basis_now, sigma)


def solution(mesh):
    return jax.shard_map(
        body,
        mesh=mesh,
        in_specs=(
            P(None, "gx", "sec", None),
            P("gx", "sec"),
            P(),
            P(),
            P(),
            P(("gx", "sec"), None, None, None),
            P(),
        ),
        out_specs=(P(None, "gx", "sec", None), P(("gx", "sec"), None, None, None), P()),
        check_vma=False,
    )
```

profile of v0, /device:TPU:6, one launch (start us, length us, event | category | flops | bytes accessed | tf_op | source)
XLA Modules:
  0.0 627.0 jit_solution(13930910843129405325)
XLA Ops:
  11.1 7.9 %collective-permute-start.1 = (bf16[1,8,128]{2,1,0:T(8,128)(2,1)}, bf16[1,8,128]{2,1,0:T(8,128)(2,1)}, u32[]{:S(2)}, u32[]{:S(2)}) collective-permute-start(bf16[1,8,128]{2,1,0:T(8,128)(2,1)} %get-tuple-element.186), channel_id=1, source_target_pairs={{8,0},{16,8},{24,16},{32,24},{40,32},{48,40},{56,48},{64,56},{72,6... | collective-permute-start | bytes 6152 | tf_op jit(solution)/shard_map/ppermute | solution.py:22
  22.6 6.7 %collective-permute-start.5 = (bf16[8,1,8,128]{3,2,0,1:T(8,128)(2,1)}, bf16[8,1,8,128]{3,2,0,1:T(8,128)(2,1)}, u32[]{:S(2)}, u32[]{:S(2)}) collective-permute-start(bf16[8,1,8,128]{3,2,0,1:T(8,128)(2,1)} %get-tuple-element.160), channel_id=1, source_target_pairs={{8,0},{16,8},{24,16},{32,24},{40,32},{48,40},{56,48},{64,56},{72,6... | collective-permute-start | bytes 49160 | tf_op jit(solution)/shard_map/ppermute | solution.py:22
  34.6 5.5 fusion.8
  51.2 6.4 %collective-permute-start.21 = (bf16[8,1,8,128]{3,2,0,1:T(8,128)(2,1)}, bf16[8,1,8,128]{3,2,0,1:T(8,128)(2,1)S(1)}, u32[]{:S(2)}, u32[]{:S(2)}) collective-permute-start(bf16[8,1,8,128]{3,2,0,1:T(8,128)(2,1)} %get-tuple-element.168), channel_id=1, source_target_pairs={{8,0},{16,8},{24,16},{32,24},{40,32},{48,40},{56,48},{64,56},{72,6... | collective-permute-start | bytes 49160 | tf_op jit(solution)/shard_map/ppermute | solution.py:22
  59.5 4.3 collective-permute-start.6
  65.2 4.5 collective-permute-start.22
  79.1 6.7 %collective-permute-start.9 = (bf16[8,1,8,128]{3,2,0,1:T(8,128)(2,1)S(1)}, bf16[8,1,8,128]{3,2,0,1:T(8,128)(2,1)S(1)}, u32[]{:S(2)}, u32[]{:S(2)}) collective-permute-start(bf16[8,1,8,128]{3,2,0,1:T(8,128)(2,1)S(1)} %get-tuple-element.158), channel_id=1, source_target_pairs={{8,0},{16,8},{24,16},{32,24},{40,32},{48,40},{56,48},{64,56},{72,6... | collective-permute-start | bytes 49160 | tf_op jit(solution)/shard_map/ppermute | solution.py:22
  87.9 6.7 %collective-permute-start.25 = (bf16[8,1,8,128]{3,2,0,1:T(8,128)(2,1)S(1)}, bf16[8,1,8,128]{3,2,0,1:T(8,128)(2,1)S(1)}, u32[]{:S(2)}, u32[]{:S(2)}) collective-permute-start(bf16[8,1,8,128]{3,2,0,1:T(8,128)(2,1)S(1)} %get-tuple-element.166), channel_id=1, source_target_pairs={{8,0},{16,8},{24,16},{32,24},{40,32},{48,40},{56,48},{64,56},{72,6... | collective-permute-start | bytes 49160 | tf_op jit(solution)/shard_map/ppermute | solution.py:22
  99.7 6.7 %collective-permute-start.26 = (bf16[8,10,1,128]{3,2,0,1:T(2,128)(2,1)S(1)}, bf16[8,10,1,128]{3,2,0,1:T(2,128)(2,1)S(1)}, u32[]{:S(2)}, u32[]{:S(2)}) collective-permute-start(bf16[8,10,1,128]{3,2,0,1:T(2,128)(2,1)S(1)} %get-tuple-element.149), channel_id=1, source_target_pairs={{0,1},{1,2},{2,3},{3,4},{4,5},{5,6},{6,7},{8,9},{9,10},{10,11},{11... | collective-permute-start | bytes 61448 | tf_op jit(solution)/shard_map/ppermute | solution.py:19
  109.5 4.9 collective-permute-done.27
  117.9 6.7 %collective-permute-start.13 = (bf16[8,1,8,128]{3,2,0,1:T(8,128)(2,1)S(1)}, bf16[8,1,8,128]{3,2,0,1:T(8,128)(2,1)S(1)}, u32[]{:S(2)}, u32[]{:S(2)}) collective-permute-start(bf16[8,1,8,128]{3,2,0,1:T(8,128)(2,1)S(1)} %get-tuple-element.156), channel_id=1, source_target_pairs={{8,0},{16,8},{24,16},{32,24},{40,32},{48,40},{56,48},{64,56},{72,6... | collective-permute-start | bytes 49160 | tf_op jit(solution)/shard_map/ppermute | solution.py:22
  126.6 6.7 %collective-permute-start.29 = (bf16[8,1,8,128]{3,2,0,1:T(8,128)(2,1)S(1)}, bf16[8,1,8,128]{3,2,0,1:T(8,128)(2,1)S(1)}, u32[]{:S(2)}, u32[]{:S(2)}) collective-permute-start(bf16[8,1,8,128]{3,2,0,1:T(8,128)(2,1)S(1)} %get-tuple-element.164), channel_id=1, source_target_pairs={{8,0},{16,8},{24,16},{32,24},{40,32},{48,40},{56,48},{64,56},{72,6... | collective-permute-start | bytes 49160 | tf_op jit(solution)/shard_map/ppermute | solution.py:22
  138.8 6.0 collective-permute-start.30
  147.8 5.1 collective-permute-done.31
  156.4 6.7 %collective-permute-start.17 = (bf16[8,1,8,128]{3,2,0,1:T(8,128)(2,1)S(1)}, bf16[8,1,8,128]{3,2,0,1:T(8,128)(2,1)S(1)}, u32[]{:S(2)}, u32[]{:S(2)}) collective-permute-start(bf16[8,1,8,128]{3,2,0,1:T(8,128)(2,1)S(1)} %get-tuple-element.154), channel_id=1, source_target_pairs={{8,0},{16,8},{24,16},{32,24},{40,32},{48,40},{56,48},{64,56},{72,6... | collective-permute-start | bytes 49160 | tf_op jit(solution)/shard_map/ppermute | solution.py:22
  165.2 6.7 %collective-permute-start.33 = (bf16[8,1,8,128]{3,2,0,1:T(8,128)(2,1)S(1)}, bf16[8,1,8,128]{3,2,0,1:T(8,128)(2,1)S(1)}, u32[]{:S(2)}, u32[]{:S(2)}) collective-permute-start(bf16[8,1,8,128]{3,2,0,1:T(8,128)(2,1)S(1)} %get-tuple-element.162), channel_id=1, source_target_pairs={{8,0},{16,8},{24,16},{32,24},{40,32},{48,40},{56,48},{64,56},{72,6... | collective-permute-start | bytes 49160 | tf_op jit(solution)/shard_map/ppermute | solution.py:22
  177.2 4.7 collective-permute-start.34
  185.4 10.4 %all-to-all-start = ((bf16[32,8,8,128]{3,2,0,1:T(8,128)(2,1)}), bf16[32,8,8,128]{3,2,0,1:T(8,128)(2,1)S(1)}, u32[]{:S(2)}, u32[]{:S(2)}) async-start(bf16[32,8,8,128]{3,2,0,1:T(8,128)(2,1)} %pad_maximum_fusion.1), calls=%async_computation | async-start | bytes 1048576 | tf_op jit(solution)/shard_map/all_to_all | solution.py:165
  198.2 5.9 all-to-all-done
  208.5 7.3 %all-to-all-done.1 = bf16[32,8,8,128]{3,2,0,1:T(8,128)(2,1)S(1)} async-done(((bf16[32,8,8,128]{3,2,0,1:T(8,128)(2,1)}), bf16[32,8,8,128]{3,2,0,1:T(8,128)(2,1)S(1)}, u32[]{:S(2)}, u32[]{:S(2)}) %all-to-all-start.1) | async-done | bytes 524320 | tf_op jit(solution)/shard_map/all_to_all | solution.py:165
  220.6 249.7 %all-reduce.23.cloned.1.call-done = f32[320,384]{1,0:T(8,128)} async-done(((f32[320,384]{1,0:T(8,128)}), f32[320,384]{1,0:T(8,128)}) %all-reduce.23.cloned.1.call-update) | async-done | bytes 491536 | tf_op jit(solution)/shard_map/psum | solution.py:183
  474.5 11.7 %cholesky.130 = f32[128,128]{1,0:T(8,128)S(1)} custom-call(f32[128,128]{1,0:T(8,128)S(1)} %cholesky.194), custom_call_target="Cholesky" | custom-call | tf_op jit(solution)/shard_map/jit(cholesky)/cholesky | solution.py:67
  486.9 9.8 %custom-call.13 = f32[1,128,128]{1,2,0:T(8,128)S(1)} custom-call(f32[1,128,128]{2,1,0:T(8,128)S(1)} %get-tuple-element.182), custom_call_target="InvertDiagBlocksLowerTriangular" | custom-call | tf_op jit(solution)/shard_map/jit(cholesky)/cholesky | solution.py:67
  497.2 11.9 %cholesky.147 = f32[128,128]{1,0:T(8,128)S(1)} custom-call(f32[128,128]{1,0:T(8,128)S(1)} %convolution_subtract_fusion.3), custom_call_target="Cholesky" | custom-call | tf_op jit(solution)/shard_map/jit(cholesky)/cholesky | solution.py:67
  511.3 4.1 while.4
  515.4 19.7 %custom-call.14 = f32[2,128,128]{1,2,0:T(8,128)S(1)} custom-call(f32[2,128,128]{2,1,0:T(8,128)S(1)} %get-tuple-element.19), custom_call_target="InvertDiagBlocksLowerTriangular" | custom-call | tf_op jit(solution)/shard_map/triangular_solve/custom-call.0 | solution.py:69
  542.5 11.7 %cholesky.164 = f32[128,128]{1,0:T(8,128)S(1)} custom-call(f32[128,128]{1,0:T(8,128)S(1)} %cholesky.197), custom_call_target="Cholesky" | custom-call | tf_op jit(solution)/shard_map/jit(cholesky)/cholesky | solution.py:67
  554.9 9.8 %custom-call.15 = f32[1,128,128]{1,2,0:T(8,128)S(1)} custom-call(f32[1,128,128]{2,1,0:T(8,128)S(1)} %get-tuple-element.178), custom_call_target="InvertDiagBlocksLowerTriangular" | custom-call | tf_op jit(solution)/shard_map/jit(cholesky)/cholesky | solution.py:67
  565.2 11.9 %cholesky.181 = f32[128,128]{1,0:T(8,128)S(1)} custom-call(f32[128,128]{1,0:T(8,128)S(1)} %convolution_subtract_fusion.2), custom_call_target="Cholesky" | custom-call | tf_op jit(solution)/shard_map/jit(cholesky)/cholesky | solution.py:67
  579.2 4.1 while.5
  583.4 19.7 %custom-call.16 = f32[2,128,128]{1,2,0:T(8,128)S(1)} custom-call(f32[2,128,128]{2,1,0:T(8,128)S(1)} %get-tuple-element.20), custom_call_target="InvertDiagBlocksLowerTriangular" | custom-call | tf_op jit(solution)/shard_map/triangular_solve/custom-call.0 | solution.py:69
  613.0 6.4 %copy.82 = bf16[8192,256]{1,0:T(8,128)(2,1)} copy(bf16[8192,256]{0,1:T(8,128)(2,1)} %fusion) | data formatting | bytes 8388608
  (274 shorter events, 120.0 us)
Async XLA Ops:
  9.1 34.6 %collective-permute-start = (bf16[1,8,128]{2,1,0:T(8,128)(2,1)}, bf16[1,8,128]{2,1,0:T(8,128)(2,1)}, u32[]{:S(2)}, u32[]{:S(2)}) collective-permute-start(bf16[1,8,128]{2,1,0:T(8,128)(2,1)} %get-tuple-element.185), channel_id=1, source_target_pairs={{0,8},{8,16},{16,24},{24,32},{32,40},{40,48},{48,56},{56,64},{64,7... | collective-permute-start | bytes 6152 | tf_op jit(solution)/shard_map/ppermute | solution.py:19
  11.1 32.7 %collective-permute-start.1 = (bf16[1,8,128]{2,1,0:T(8,128)(2,1)}, bf16[1,8,128]{2,1,0:T(8,128)(2,1)}, u32[]{:S(2)}, u32[]{:S(2)}) collective-permute-start(bf16[1,8,128]{2,1,0:T(8,128)(2,1)} %get-tuple-element.186), channel_id=1, source_target_pairs={{8,0},{16,8},{24,16},{32,24},{40,32},{48,40},{56,48},{64,56},{72,6... | collective-permute-start | bytes 6152 | tf_op jit(solution)/shard_map/ppermute | solution.py:22
  20.7 38.0 %collective-permute-start.4 = (bf16[8,1,8,128]{3,2,0,1:T(8,128)(2,1)}, bf16[8,1,8,128]{3,2,0,1:T(8,128)(2,1)S(1)}, u32[]{:S(2)}, u32[]{:S(2)}) collective-permute-start(bf16[8,1,8,128]{3,2,0,1:T(8,128)(2,1)} %get-tuple-element.159), channel_id=1, source_target_pairs={{0,8},{8,16},{16,24},{24,32},{32,40},{40,48},{48,56},{56,64},{64,7... | collective-permute-start | bytes 49160 | tf_op jit(solution)/shard_map/ppermute | solution.py:19
  22.6 36.1 %collective-permute-start.5 = (bf16[8,1,8,128]{3,2,0,1:T(8,128)(2,1)}, bf16[8,1,8,128]{3,2,0,1:T(8,128)(2,1)}, u32[]{:S(2)}, u32[]{:S(2)}) collective-permute-start(bf16[8,1,8,128]{3,2,0,1:T(8,128)(2,1)} %get-tuple-element.160), channel_id=1, source_target_pairs={{8,0},{16,8},{24,16},{32,24},{40,32},{48,40},{56,48},{64,56},{72,6... | collective-permute-start | bytes 49160 | tf_op jit(solution)/shard_map/ppermute | solution.py:22
  29.9 35.2 %collective-permute-start.20 = (bf16[8,1,8,128]{3,2,0,1:T(8,128)(2,1)}, bf16[8,1,8,128]{3,2,0,1:T(8,128)(2,1)S(1)}, u32[]{:S(2)}, u32[]{:S(2)}) collective-permute-start(bf16[8,1,8,128]{3,2,0,1:T(8,128)(2,1)} %get-tuple-element.167), channel_id=1, source_target_pairs={{0,8},{8,16},{16,24},{24,32},{32,40},{40,48},{48,56},{56,64},{64,7... | collective-permute-start | bytes 49160 | tf_op jit(solution)/shard_map/ppermute | solution.py:19
  48.1 9.4 %collective-permute-start.3 = (bf16[10,1,128]{2,1,0:T(2,128)(2,1)S(1)}, bf16[10,1,128]{2,1,0:T(2,128)(2,1)S(1)}, u32[]{:S(2)}, u32[]{:S(2)}) collective-permute-start(bf16[10,1,128]{2,1,0:T(2,128)(2,1)S(1)} %get-tuple-element.184), channel_id=1, source_target_pairs={{1,0},{2,1},{3,2},{4,3},{5,4},{6,5},{7,6},{9,8},{10,9},{11,10},{12... | collective-permute-start | bytes 7688 | tf_op jit(solution)/shard_map/ppermute | solution.py:22
  51.2 13.9 %collective-permute-start.21 = (bf16[8,1,8,128]{3,2,0,1:T(8,128)(2,1)}, bf16[8,1,8,128]{3,2,0,1:T(8,128)(2,1)S(1)}, u32[]{:S(2)}, u32[]{:S(2)}) collective-permute-start(bf16[8,1,8,128]{3,2,0,1:T(8,128)(2,1)} %get-tuple-element.168), channel_id=1, source_target_pairs={{8,0},{16,8},{24,16},{32,24},{40,32},{48,40},{56,48},{64,56},{72,6... | collective-permute-start | bytes 49160 | tf_op jit(solution)/shard_map/ppermute | solution.py:22
  59.5 11.5 %collective-permute-start.6 = (bf16[8,10,1,128]{3,2,0,1:T(2,128)(2,1)S(1)}, bf16[8,10,1,128]{3,2,0,1:T(2,128)(2,1)S(1)}, u32[]{:S(2)}, u32[]{:S(2)}) collective-permute-start(bf16[8,10,1,128]{3,2,0,1:T(2,128)(2,1)S(1)} %get-tuple-element.143), channel_id=1, source_target_pairs={{0,1},{1,2},{2,3},{3,4},{4,5},{5,6},{6,7},{8,9},{9,10},{10,11},{11... | collective-permute-start | bytes 61448 | tf_op jit(solution)/shard_map/ppermute | solution.py:19
  65.2 9.2 %collective-permute-start.22 = (bf16[8,10,1,128]{3,2,0,1:T(2,128)(2,1)S(1)}, bf16[8,10,1,128]{3,2,0,1:T(2,128)(2,1)S(1)}, u32[]{:S(2)}, u32[]{:S(2)}) collective-permute-start(bf16[8,10,1,128]{3,2,0,1:T(2,128)(2,1)S(1)} %get-tuple-element.151), channel_id=1, source_target_pairs={{0,1},{1,2},{2,3},{3,4},{4,5},{5,6},{6,7},{8,9},{9,10},{10,11},{11... | collective-permute-start | bytes 61448 | tf_op jit(solution)/shard_map/ppermute | solution.py:19
  77.2 17.5 %collective-permute-start.8 = (bf16[8,1,8,128]{3,2,0,1:T(8,128)(2,1)S(1)}, bf16[8,1,8,128]{3,2,0,1:T(8,128)(2,1)S(1)}, u32[]{:S(2)}, u32[]{:S(2)}) collective-permute-start(bf16[8,1,8,128]{3,2,0,1:T(8,128)(2,1)S(1)} %get-tuple-element.157), channel_id=1, source_target_pairs={{0,8},{8,16},{16,24},{24,32},{32,40},{40,48},{48,56},{56,64},{64,7... | collective-permute-start | bytes 49160 | tf_op jit(solution)/shard_map/ppermute | solution.py:19
  79.1 15.5 %collective-permute-start.9 = (bf16[8,1,8,128]{3,2,0,1:T(8,128)(2,1)S(1)}, bf16[8,1,8,128]{3,2,0,1:T(8,128)(2,1)S(1)}, u32[]{:S(2)}, u32[]{:S(2)}) collective-permute-start(bf16[8,1,8,128]{3,2,0,1:T(8,128)(2,1)S(1)} %get-tuple-element.158), channel_id=1, source_target_pairs={{8,0},{16,8},{24,16},{32,24},{40,32},{48,40},{56,48},{64,56},{72,6... | collective-permute-start | bytes 49160 | tf_op jit(solution)/shard_map/ppermute | solution.py:22
  85.9 13.6 %collective-permute-start.24 = (bf16[8,1,8,128]{3,2,0,1:T(8,128)(2,1)S(1)}, bf16[8,1,8,128]{3,2,0,1:T(8,128)(2,1)S(1)}, u32[]{:S(2)}, u32[]{:S(2)}) collective-permute-start(bf16[8,1,8,128]{3,2,0,1:T(8,128)(2,1)S(1)} %get-tuple-element.165), channel_id=1, source_target_pairs={{0,8},{8,16},{16,24},{24,32},{32,40},{40,48},{48,56},{56,64},{64,7... | collective-permute-start | bytes 49160 | tf_op jit(solution)/shard_map/ppermute | solution.py:19
  87.9 11.7 %collective-permute-start.25 = (bf16[8,1,8,128]{3,2,0,1:T(8,128)(2,1)S(1)}, bf16[8,1,8,128]{3,2,0,1:T(8,128)(2,1)S(1)}, u32[]{:S(2)}, u32[]{:S(2)}) collective-permute-start(bf16[8,1,8,128]{3,2,0,1:T(8,128)(2,1)S(1)} %get-tuple-element.166), channel_id=1, source_target_pairs={{8,0},{16,8},{24,16},{32,24},{40,32},{48,40},{56,48},{64,56},{72,6... | collective-permute-start | bytes 49160 | tf_op jit(solution)/shard_map/ppermute | solution.py:22
  94.7 13.1 %collective-permute-start.10 = (bf16[8,10,1,128]{3,2,0,1:T(2,128)(2,1)S(1)}, bf16[8,10,1,128]{3,2,0,1:T(2,128)(2,1)S(1)}, u32[]{:S(2)}, u32[]{:S(2)}) collective-permute-start(bf16[8,10,1,128]{3,2,0,1:T(2,128)(2,1)S(1)} %get-tuple-element.141), channel_id=1, source_target_pairs={{0,1},{1,2},{2,3},{3,4},{4,5},{5,6},{6,7},{8,9},{9,10},{10,11},{11... | collective-permute-start | bytes 61448 | tf_op jit(solution)/shard_map/ppermute | solution.py:19
  98.3 9.5 %collective-permute-start.11 = (bf16[8,10,1,128]{3,2,0,1:T(2,128)(2,1)S(1)}, bf16[8,10,1,128]{3,2,0,1:T(2,128)(2,1)S(1)}, u32[]{:S(2)}, u32[]{:S(2)}) collective-permute-start(bf16[8,10,1,128]{3,2,0,1:T(2,128)(2,1)S(1)} %get-tuple-element.142), channel_id=1, source_target_pairs={{1,0},{2,1},{3,2},{4,3},{5,4},{6,5},{7,6},{9,8},{10,9},{11,10},{12... | collective-permute-start | bytes 61448 | tf_op jit(solution)/shard_map/ppermute | solution.py:22
  99.7 9.8 %collective-permute-start.26 = (bf16[8,10,1,128]{3,2,0,1:T(2,128)(2,1)S(1)}, bf16[8,10,1,128]{3,2,0,1:T(2,128)(2,1)S(1)}, u32[]{:S(2)}, u32[]{:S(2)}) collective-permute-start(bf16[8,10,1,128]{3,2,0,1:T(2,128)(2,1)S(1)} %get-tuple-element.149), channel_id=1, source_target_pairs={{0,1},{1,2},{2,3},{3,4},{4,5},{5,6},{6,7},{8,9},{9,10},{10,11},{11... | collective-permute-start | bytes 61448 | tf_op jit(solution)/shard_map/ppermute | solution.py:19
  116.0 17.5 %collective-permute-start.12 = (bf16[8,1,8,128]{3,2,0,1:T(8,128)(2,1)S(1)}, bf16[8,1,8,128]{3,2,0,1:T(8,128)(2,1)S(1)}, u32[]{:S(2)}, u32[]{:S(2)}) collective-permute-start(bf16[8,1,8,128]{3,2,0,1:T(8,128)(2,1)S(1)} %get-tuple-element.155), channel_id=1, source_target_pairs={{0,8},{8,16},{16,24},{24,32},{32,40},{40,48},{48,56},{56,64},{64,7... | collective-permute-start | bytes 49160 | tf_op jit(solution)/shard_map/ppermute | solution.py:19
  117.9 15.5 %collective-permute-start.13 = (bf16[8,1,8,128]{3,2,0,1:T(8,128)(2,1)S(1)}, bf16[8,1,8,128]{3,2,0,1:T(8,128)(2,1)S(1)}, u32[]{:S(2)}, u32[]{:S(2)}) collective-permute-start(bf16[8,1,8,128]{3,2,0,1:T(8,128)(2,1)S(1)} %get-tuple-element.156), channel_id=1, source_target_pairs={{8,0},{16,8},{24,16},{32,24},{40,32},{48,40},{56,48},{64,56},{72,6... | collective-permute-start | bytes 49160 | tf_op jit(solution)/shard_map/ppermute | solution.py:22
  124.7 14.0 %collective-permute-start.28 = (bf16[8,1,8,128]{3,2,0,1:T(8,128)(2,1)S(1)}, bf16[8,1,8,128]{3,2,0,1:T(8,128)(2,1)S(1)}, u32[]{:S(2)}, u32[]{:S(2)}) collective-permute-start(bf16[8,1,8,128]{3,2,0,1:T(8,128)(2,1)S(1)} %get-tuple-element.163), channel_id=1, source_target_pairs={{0,8},{8,16},{16,24},{24,32},{32,40},{40,48},{48,56},{56,64},{64,7... | collective-permute-start | bytes 49160 | tf_op jit(solution)/shard_map/ppermute | solution.py:19
  126.6 12.1 %collective-permute-start.29 = (bf16[8,1,8,128]{3,2,0,1:T(8,128)(2,1)S(1)}, bf16[8,1,8,128]{3,2,0,1:T(8,128)(2,1)S(1)}, u32[]{:S(2)}, u32[]{:S(2)}) collective-permute-start(bf16[8,1,8,128]{3,2,0,1:T(8,128)(2,1)S(1)} %get-tuple-element.164), channel_id=1, source_target_pairs={{8,0},{16,8},{24,16},{32,24},{40,32},{48,40},{56,48},{64,56},{72,6... | collective-permute-start | bytes 49160 | tf_op jit(solution)/shard_map/ppermute | solution.py:22
  133.5 12.6 %collective-permute-start.14 = (bf16[8,10,1,128]{3,2,0,1:T(2,128)(2,1)S(1)}, bf16[8,10,1,128]{3,2,0,1:T(2,128)(2,1)S(1)}, u32[]{:S(2)}, u32[]{:S(2)}) collective-permute-start(bf16[8,10,1,128]{3,2,0,1:T(2,128)(2,1)S(1)} %get-tuple-element.139), channel_id=1, source_target_pairs={{0,1},{1,2},{2,3},{3,4},{4,5},{5,6},{6,7},{8,9},{9,10},{10,11},{11... | collective-permute-start | bytes 61448 | tf_op jit(solution)/shard_map/ppermute | solution.py:19
  138.8 9.0 %collective-permute-start.30 = (bf16[8,10,1,128]{3,2,0,1:T(2,128)(2,1)S(1)}, bf16[8,10,1,128]{3,2,0,1:T(2,128)(2,1)S(1)}, u32[]{:S(2)}, u32[]{:S(2)}) collective-permute-start(bf16[8,10,1,128]{3,2,0,1:T(2,128)(2,1)S(1)} %get-tuple-element.147), channel_id=1, source_target_pairs={{0,1},{1,2},{2,3},{3,4},{4,5},{5,6},{6,7},{8,9},{9,10},{10,11},{11... | collective-permute-start | bytes 61448 | tf_op jit(solution)/shard_map/ppermute | solution.py:19
  154.5 17.3 %collective-permute-start.16 = (bf16[8,1,8,128]{3,2,0,1:T(8,128)(2,1)S(1)}, bf16[8,1,8,128]{3,2,0,1:T(8,128)(2,1)S(1)}, u32[]{:S(2)}, u32[]{:S(2)}) collective-permute-start(bf16[8,1,8,128]{3,2,0,1:T(8,128)(2,1)S(1)} %get-tuple-element.153), channel_id=1, source_target_pairs={{0,8},{8,16},{16,24},{24,32},{32,40},{40,48},{48,56},{56,64},{64,7... | collective-permute-start | bytes 49160 | tf_op jit(solution)/shard_map/ppermute | solution.py:19
  156.4 15.4 %collective-permute-start.17 = (bf16[8,1,8,128]{3,2,0,1:T(8,128)(2,1)S(1)}, bf16[8,1,8,128]{3,2,0,1:T(8,128)(2,1)S(1)}, u32[]{:S(2)}, u32[]{:S(2)}) collective-permute-start(bf16[8,1,8,128]{3,2,0,1:T(8,128)(2,1)S(1)} %get-tuple-element.154), channel_id=1, source_target_pairs={{8,0},{16,8},{24,16},{32,24},{40,32},{48,40},{56,48},{64,56},{72,6... | collective-permute-start | bytes 49160 | tf_op jit(solution)/shard_map/ppermute | solution.py:22
  163.2 13.9 %collective-permute-start.32 = (bf16[8,1,8,128]{3,2,0,1:T(8,128)(2,1)S(1)}, bf16[8,1,8,128]{3,2,0,1:T(8,128)(2,1)S(1)}, u32[]{:S(2)}, u32[]{:S(2)}) collective-permute-start(bf16[8,1,8,128]{3,2,0,1:T(8,128)(2,1)S(1)} %get-tuple-element.161), channel_id=1, source_target_pairs={{0,8},{8,16},{16,24},{24,32},{32,40},{40,48},{48,56},{56,64},{64,7... | collective-permute-start | bytes 49160 | tf_op jit(solution)/shard_map/ppermute | solution.py:19
  165.2 12.0 %collective-permute-start.33 = (bf16[8,1,8,128]{3,2,0,1:T(8,128)(2,1)S(1)}, bf16[8,1,8,128]{3,2,0,1:T(8,128)(2,1)S(1)}, u32[]{:S(2)}, u32[]{:S(2)}) collective-permute-start(bf16[8,1,8,128]{3,2,0,1:T(8,128)(2,1)S(1)} %get-tuple-element.162), channel_id=1, source_target_pairs={{8,0},{16,8},{24,16},{32,24},{40,32},{48,40},{56,48},{64,56},{72,6... | collective-permute-start | bytes 49160 | tf_op jit(solution)/shard_map/ppermute | solution.py:22
  171.9 11.3 %collective-permute-start.18 = (bf16[8,10,1,128]{3,2,0,1:T(2,128)(2,1)S(1)}, bf16[8,10,1,128]{3,2,0,1:T(2,128)(2,1)S(1)}, u32[]{:S(2)}, u32[]{:S(2)}) collective-permute-start(bf16[8,10,1,128]{3,2,0,1:T(2,128)(2,1)S(1)} %get-tuple-element.137), channel_id=1, source_target_pairs={{0,1},{1,2},{2,3},{3,4},{4,5},{5,6},{6,7},{8,9},{9,10},{10,11},{11... | collective-permute-start | bytes 61448 | tf_op jit(solution)/shard_map/ppermute | solution.py:19
  177.2 18.7 %collective-permute-start.34 = (bf16[8,10,1,128]{3,2,0,1:T(2,128)(2,1)S(1)}, bf16[8,10,1,128]{3,2,0,1:T(2,128)(2,1)S(1)}, u32[]{:S(2)}, u32[]{:S(2)}) collective-permute-start(bf16[8,10,1,128]{3,2,0,1:T(2,128)(2,1)S(1)} %get-tuple-element.145), channel_id=1, source_target_pairs={{0,1},{1,2},{2,3},{3,4},{4,5},{5,6},{6,7},{8,9},{9,10},{10,11},{11... | collective-permute-start | bytes 61448 | tf_op jit(solution)/shard_map/ppermute | solution.py:19
  181.9 14.1 %collective-permute-start.35 = (bf16[8,10,1,128]{3,2,0,1:T(2,128)(2,1)S(1)}, bf16[8,10,1,128]{3,2,0,1:T(2,128)(2,1)S(1)}, u32[]{:S(2)}, u32[]{:S(2)}) collective-permute-start(bf16[8,10,1,128]{3,2,0,1:T(2,128)(2,1)S(1)} %get-tuple-element.146), channel_id=1, source_target_pairs={{1,0},{2,1},{3,2},{4,3},{5,4},{6,5},{7,6},{9,8},{10,9},{11,10},{12... | collective-permute-start | bytes 61448 | tf_op jit(solution)/shard_map/ppermute | solution.py:22
  185.4 18.6 %all-to-all-start = ((bf16[32,8,8,128]{3,2,0,1:T(8,128)(2,1)}), bf16[32,8,8,128]{3,2,0,1:T(8,128)(2,1)S(1)}, u32[]{:S(2)}, u32[]{:S(2)}) async-start(bf16[32,8,8,128]{3,2,0,1:T(8,128)(2,1)} %pad_maximum_fusion.1), calls=%async_computation | async-start | bytes 1048576 | tf_op jit(solution)/shard_map/all_to_all | solution.py:165
  204.1 11.7 %all-to-all-start.1 = ((bf16[32,8,8,128]{3,2,0,1:T(8,128)(2,1)}), bf16[32,8,8,128]{3,2,0,1:T(8,128)(2,1)S(1)}, u32[]{:S(2)}, u32[]{:S(2)}) async-start(bf16[32,8,8,128]{3,2,0,1:T(8,128)(2,1)} %pad_maximum_fusion.2), calls=%async_computation.1 | async-start | bytes 1048576 | tf_op jit(solution)/shard_map/all_to_all | solution.py:165
  207.6 262.7 %all-reduce.23.cloned.1.call-start = ((), (), s32[]{:S(2)}) async-start(), calls=%async_computation.2 | async-start | bytes 983040 | tf_op jit(solution)/shard_map/psum | solution.py:183
  (21 other events, 270.8 us)
Sparse Core Ops, SparseCore 0:
  219.8 250.5 all-reduce.22
where the time goes:
time: 635 us; the launch traced here: 627 us
  waiting for transfers between devices  274 us (43%)
  starting transfers between devices  145 us (23%)
  other arithmetic  131 us (21%)
  matrix products  30.2 us (5%)
  local copies, waits for them, and re-layouts  27.9 us (4%)
  between operations  18.7 us (3%)
    psum x1, waiting for transfers between devices, body(): whole = lax.psum(local, ('gx', 'sec')) / rows_total  250 us
    ppermute x18, starting transfers between devices, with_halo(): lax.ppermute(lax.slice_in_dim(block, 0, width, axis=dim), axis, backward)  72.6 us
    another operation x14, other arithmetic, batch_update(): factor = jnp.linalg.cholesky(inner)  69.7 us
    ppermute x18, starting transfers between devices, with_halo(): lax.ppermute(lax.slice_in_dim(block, block.shape[dim] - width, None, axis...  58.3 us
    another operation x5, other arithmetic, batch_update(): lax.linalg.triangular_solve(factor, eye, left_side=True, lower=True)  39.4 us
    all_to_all x2, starting transfers between devices, body(): lax.all_to_all(stacked, 'sec', split_axis=1, concat_axis=2, tiled=True)  13.9 us
    all_to_all x2, waiting for transfers between devices, body(): lax.all_to_all(stacked, 'sec', split_axis=1, concat_axis=2, tiled=True)  13.2 us
  transfers between devices with their start and end apart: 39, of which 6 were waited for; matrix products, arithmetic and copies ran while one was open for 5% of the time, Pallas kernels for 0%

commit v1 on v0

--- a/solution.py
+++ b/solution.py
@@ -180,7 +180,7 @@
         ],
         1,
     )
-    whole = lax.psum(local, ("gx", "sec")) / rows_total
+    whole = lax.psum(lax.psum(local, "sec"), "gx") / rows_total
     w0, w1, w2, sigma = small_algebra(
         whole[:count, :count],
         whole[count:, :count],

time: 635 us -> 741 us (1.17)
  the two profiles are of different devices: /device:TPU:6 before, /device:TPU:8 now
where the time goes in v1:
time: 741 us; the launch traced here: 731 us
  waiting for transfers between devices  394 us (53%)
  starting transfers between devices  135 us (18%)
  other arithmetic  126 us (17%)
  matrix products  30.2 us (4%)
  local copies, waits for them, and re-layouts  26.3 us (4%)
  between operations  18.6 us (3%)
    psum x2, waiting for transfers between devices, body(): whole = lax.psum(lax.psum(local, 'sec'), 'gx') / rows_total  373 us
    ppermute x18, starting transfers between devices, with_halo(): lax.ppermute(lax.slice_in_dim(block, block.shape[dim] - width, None, axis...  91.3 us
    another operation x14, other arithmetic, batch_update(): factor = jnp.linalg.cholesky(inner)  69.6 us
    another operation x5, other arithmetic, batch_update(): lax.linalg.triangular_solve(factor, eye, left_side=True, lower=True)  39.4 us
    ppermute x18, starting transfers between devices, with_halo(): lax.ppermute(lax.slice_in_dim(block, 0, width, axis=dim), axis, backward)  30.1 us
  transfers between devices with their start and end apart: 40, of which 8 were waited for; matrix products, arithmetic and copies ran while one was open for 4% of the time, Pallas kernels for 0%

profile of v1, /device:TPU:8, one launch (start us, length us, event | category | flops | bytes accessed | tf_op | source)
XLA Modules:
  0.0 730.9 jit_solution(17191108733195640067)
XLA Ops:
  12.7 6.1 collective-permute-start.4
  20.1 5.2 collective-permute-start.20
  28.1 5.5 fusion.8
  52.8 4.9 collective-permute-start.22
  68.7 7.2 collective-permute-start.24
  77.4 5.6 collective-permute-start.10
  85.0 6.0 collective-permute-start.26
  98.6 4.0 collective-permute-start.12
  104.1 8.4 %collective-permute-start.28 = (bf16[8,1,8,128]{3,2,0,1:T(8,128)(2,1)S(1)}, bf16[8,1,8,128]{3,2,0,1:T(8,128)(2,1)S(1)}, u32[]{:S(2)}, u32[]{:S(2)}) collective-permute-start(bf16[8,1,8,128]{3,2,0,1:T(8,128)(2,1)S(1)} %get-tuple-element.163), channel_id=1, source_target_pairs={{0,8},{8,16},{16,24},{24,32},{32,40},{40,48},{48,56},{56,64},{64,7... | collective-permute-start | bytes 49160 | tf_op jit(solution)/shard_map/ppermute | solution.py:19
  114.0 4.7 collective-permute-start.14
  120.7 6.0 collective-permute-start.30
  134.3 4.7 collective-permute-start.16
  140.4 8.1 %collective-permute-start.32 = (bf16[8,1,8,128]{3,2,0,1:T(8,128)(2,1)S(1)}, bf16[8,1,8,128]{3,2,0,1:T(8,128)(2,1)S(1)}, u32[]{:S(2)}, u32[]{:S(2)}) collective-permute-start(bf16[8,1,8,128]{3,2,0,1:T(8,128)(2,1)S(1)} %get-tuple-element.161), channel_id=1, source_target_pairs={{0,8},{8,16},{16,24},{24,32},{32,40},{40,48},{48,56},{56,64},{64,7... | collective-permute-start | bytes 49160 | tf_op jit(solution)/shard_map/ppermute | solution.py:19
  149.9 4.0 collective-permute-start.18
  155.9 6.0 collective-permute-start.34
  166.1 7.5 %all-to-all-start = ((bf16[32,8,8,128]{3,2,0,1:T(8,128)(2,1)}), bf16[32,8,8,128]{3,2,0,1:T(8,128)(2,1)S(1)}, u32[]{:S(2)}, u32[]{:S(2)}) async-start(bf16[32,8,8,128]{3,2,0,1:T(8,128)(2,1)} %pad_maximum_fusion.1), calls=%async_computation | async-start | bytes 1048576 | tf_op jit(solution)/shard_map/all_to_all | solution.py:165
  175.9 5.8 all-to-all-done
  181.7 6.0 all-to-all-start.1
  188.1 7.9 %all-to-all-done.1 = bf16[32,8,8,128]{3,2,0,1:T(8,128)(2,1)S(1)} async-done(((bf16[32,8,8,128]{3,2,0,1:T(8,128)(2,1)}), bf16[32,8,8,128]{3,2,0,1:T(8,128)(2,1)S(1)}, u32[]{:S(2)}, u32[]{:S(2)}) %all-to-all-start.1) | async-done | bytes 524320 | tf_op jit(solution)/shard_map/all_to_all | solution.py:165
  200.4 87.3 %all-reduce.24.cloned.1.call-done = f32[320,384]{1,0:T(8,128)} async-done(((f32[320,384]{1,0:T(8,128)}), f32[320,384]{1,0:T(8,128)}) %all-reduce.24.cloned.1.call-update) | async-done | bytes 491536 | tf_op jit(solution)/shard_map/psum | solution.py:183
  288.7 286.0 %all-reduce.26.cloned.1.call-done = f32[320,384]{1,0:T(8,128)} async-done(((f32[320,384]{1,0:T(8,128)}), f32[320,384]{1,0:T(8,128)}) %all-reduce.26.cloned.1.call-update) | async-done | bytes 491536 | tf_op jit(solution)/shard_map/psum | solution.py:183
  578.9 11.7 %cholesky.130 = f32[128,128]{1,0:T(8,128)S(1)} custom-call(f32[128,128]{1,0:T(8,128)S(1)} %cholesky.194), custom_call_target="Cholesky" | custom-call | tf_op jit(solution)/shard_map/jit(cholesky)/cholesky | solution.py:67
  591.3 9.8 %custom-call.13 = f32[1,128,128]{1,2,0:T(8,128)S(1)} custom-call(f32[1,128,128]{2,1,0:T(8,128)S(1)} %get-tuple-element.182), custom_call_target="InvertDiagBlocksLowerTriangular" | custom-call | tf_op jit(solution)/shard_map/jit(cholesky)/cholesky | solution.py:67
  601.7 11.9 %cholesky.147 = f32[128,128]{1,0:T(8,128)S(1)} custom-call(f32[128,128]{1,0:T(8,128)S(1)} %convolution_subtract_fusion.3), custom_call_target="Cholesky" | custom-call | tf_op jit(solution)/shard_map/jit(cholesky)/cholesky | solution.py:67
  615.5 3.9 while.4
  619.4 19.7 %custom-call.14 = f32[2,128,128]{1,2,0:T(8,128)S(1)} custom-call(f32[2,128,128]{2,1,0:T(8,128)S(1)} %get-tuple-element.19), custom_call_target="InvertDiagBlocksLowerTriangular" | custom-call | tf_op jit(solution)/shard_map/triangular_solve/custom-call.0 | solution.py:69
  646.5 11.7 %cholesky.164 = f32[128,128]{1,0:T(8,128)S(1)} custom-call(f32[128,128]{1,0:T(8,128)S(1)} %cholesky.197), custom_call_target="Cholesky" | custom-call | tf_op jit(solution)/shard_map/jit(cholesky)/cholesky | solution.py:67
  658.8 9.8 %custom-call.15 = f32[1,128,128]{1,2,0:T(8,128)S(1)} custom-call(f32[1,128,128]{2,1,0:T(8,128)S(1)} %get-tuple-element.178), custom_call_target="InvertDiagBlocksLowerTriangular" | custom-call | tf_op jit(solution)/shard_map/jit(cholesky)/cholesky | solution.py:67
  669.2 11.9 %cholesky.181 = f32[128,128]{1,0:T(8,128)S(1)} custom-call(f32[128,128]{1,0:T(8,128)S(1)} %convolution_subtract_fusion.2), custom_call_target="Cholesky" | custom-call | tf_op jit(solution)/shard_map/jit(cholesky)/cholesky | solution.py:67
  683.1 4.0 while.5
  687.1 19.7 %custom-call.16 = f32[2,128,128]{1,2,0:T(8,128)S(1)} custom-call(f32[2,128,128]{2,1,0:T(8,128)S(1)} %get-tuple-element.20), custom_call_target="InvertDiagBlocksLowerTriangular" | custom-call | tf_op jit(solution)/shard_map/triangular_solve/custom-call.0 | solution.py:69
  716.7 6.4 copy.82
  (269 shorter events, 112.9 us)
Async XLA Ops:
  8.6 28.7 %collective-permute-start = (bf16[1,8,128]{2,1,0:T(8,128)(2,1)S(1)}, bf16[1,8,128]{2,1,0:T(8,128)(2,1)S(1)}, u32[]{:S(2)}, u32[]{:S(2)}) collective-permute-start(bf16[1,8,128]{2,1,0:T(8,128)(2,1)S(1)} %get-tuple-element.185), channel_id=1, source_target_pairs={{0,8},{8,16},{16,24},{24,32},{32,40},{40,48},{48,56},{56,64},{64,7... | collective-permute-start | bytes 6152 | tf_op jit(solution)/shard_map/ppermute | solution.py:19
  10.3 27.0 %collective-permute-start.1 = (bf16[1,8,128]{2,1,0:T(8,128)(2,1)S(1)}, bf16[1,8,128]{2,1,0:T(8,128)(2,1)S(1)}, u32[]{:S(2)}, u32[]{:S(2)}) collective-permute-start(bf16[1,8,128]{2,1,0:T(8,128)(2,1)S(1)} %get-tuple-element.186), channel_id=1, source_target_pairs={{8,0},{16,8},{24,16},{32,24},{40,32},{48,40},{56,48},{64,56},{72,6... | collective-permute-start | bytes 6152 | tf_op jit(solution)/shard_map/ppermute | solution.py:22
  12.7 34.1 %collective-permute-start.4 = (bf16[8,1,8,128]{3,2,0,1:T(8,128)(2,1)S(1)}, bf16[8,1,8,128]{3,2,0,1:T(8,128)(2,1)S(1)}, u32[]{:S(2)}, u32[]{:S(2)}) collective-permute-start(bf16[8,1,8,128]{3,2,0,1:T(8,128)(2,1)S(1)} %get-tuple-element.159), channel_id=1, source_target_pairs={{0,8},{8,16},{16,24},{24,32},{32,40},{40,48},{48,56},{56,64},{64,7... | collective-permute-start | bytes 49160 | tf_op jit(solution)/shard_map/ppermute | solution.py:19
  18.8 28.0 %collective-permute-start.5 = (bf16[8,1,8,128]{3,2,0,1:T(8,128)(2,1)S(1)}, bf16[8,1,8,128]{3,2,0,1:T(8,128)(2,1)S(1)}, u32[]{:S(2)}, u32[]{:S(2)}) collective-permute-start(bf16[8,1,8,128]{3,2,0,1:T(8,128)(2,1)S(1)} %get-tuple-element.160), channel_id=1, source_target_pairs={{8,0},{16,8},{24,16},{32,24},{40,32},{48,40},{56,48},{64,56},{72,6... | collective-permute-start | bytes 49160 | tf_op jit(solution)/shard_map/ppermute | solution.py:22
  20.1 32.6 %collective-permute-start.20 = (bf16[8,1,8,128]{3,2,0,1:T(8,128)(2,1)S(1)}, bf16[8,1,8,128]{3,2,0,1:T(8,128)(2,1)S(1)}, u32[]{:S(2)}, u32[]{:S(2)}) collective-permute-start(bf16[8,1,8,128]{3,2,0,1:T(8,128)(2,1)S(1)} %get-tuple-element.167), channel_id=1, source_target_pairs={{0,8},{8,16},{16,24},{24,32},{32,40},{40,48},{48,56},{56,64},{64,7... | collective-permute-start | bytes 49160 | tf_op jit(solution)/shard_map/ppermute | solution.py:19
  46.8 12.7 %collective-permute-start.6 = (bf16[8,10,1,128]{3,2,0,1:T(2,128)(2,1)S(1)}, bf16[8,10,1,128]{3,2,0,1:T(2,128)(2,1)S(1)}, u32[]{:S(2)}, u32[]{:S(2)}) collective-permute-start(bf16[8,10,1,128]{3,2,0,1:T(2,128)(2,1)S(1)} %get-tuple-element.143), channel_id=1, source_target_pairs={{0,1},{1,2},{2,3},{3,4},{4,5},{5,6},{6,7},{8,9},{9,10},{10,11},{11... | collective-permute-start | bytes 61448 | tf_op jit(solution)/shard_map/ppermute | solution.py:19
  50.0 9.6 %collective-permute-start.7 = (bf16[8,10,1,128]{3,2,0,1:T(2,128)(2,1)S(1)}, bf16[8,10,1,128]{3,2,0,1:T(2,128)(2,1)S(1)}, u32[]{:S(2)}, u32[]{:S(2)}) collective-permute-start(bf16[8,10,1,128]{3,2,0,1:T(2,128)(2,1)S(1)} %get-tuple-element.144), channel_id=1, source_target_pairs={{1,0},{2,1},{3,2},{4,3},{5,4},{6,5},{7,6},{9,8},{10,9},{11,10},{12... | collective-permute-start | bytes 61448 | tf_op jit(solution)/shard_map/ppermute | solution.py:22
  52.8 9.4 %collective-permute-start.22 = (bf16[8,10,1,128]{3,2,0,1:T(2,128)(2,1)S(1)}, bf16[8,10,1,128]{3,2,0,1:T(2,128)(2,1)S(1)}, u32[]{:S(2)}, u32[]{:S(2)}) collective-permute-start(bf16[8,10,1,128]{3,2,0,1:T(2,128)(2,1)S(1)} %get-tuple-element.151), channel_id=1, source_target_pairs={{0,1},{1,2},{2,3},{3,4},{4,5},{5,6},{6,7},{8,9},{9,10},{10,11},{11... | collective-permute-start | bytes 61448 | tf_op jit(solution)/shard_map/ppermute | solution.py:19
  65.2 12.2 %collective-permute-start.8 = (bf16[8,1,8,128]{3,2,0,1:T(8,128)(2,1)S(1)}, bf16[8,1,8,128]{3,2,0,1:T(8,128)(2,1)S(1)}, u32[]{:S(2)}, u32[]{:S(2)}) collective-permute-start(bf16[8,1,8,128]{3,2,0,1:T(8,128)(2,1)S(1)} %get-tuple-element.157), channel_id=1, source_target_pairs={{0,8},{8,16},{16,24},{24,32},{32,40},{40,48},{48,56},{56,64},{64,7... | collective-permute-start | bytes 49160 | tf_op jit(solution)/shard_map/ppermute | solution.py:19
  67.3 10.1 %collective-permute-start.9 = (bf16[8,1,8,128]{3,2,0,1:T(8,128)(2,1)S(1)}, bf16[8,1,8,128]{3,2,0,1:T(8,128)(2,1)S(1)}, u32[]{:S(2)}, u32[]{:S(2)}) collective-permute-start(bf16[8,1,8,128]{3,2,0,1:T(8,128)(2,1)S(1)} %get-tuple-element.158), channel_id=1, source_target_pairs={{8,0},{16,8},{24,16},{32,24},{40,32},{48,40},{56,48},{64,56},{72,6... | collective-permute-start | bytes 49160 | tf_op jit(solution)/shard_map/ppermute | solution.py:22
  68.7 16.2 %collective-permute-start.24 = (bf16[8,1,8,128]{3,2,0,1:T(8,128)(2,1)S(1)}, bf16[8,1,8,128]{3,2,0,1:T(8,128)(2,1)S(1)}, u32[]{:S(2)}, u32[]{:S(2)}) collective-permute-start(bf16[8,1,8,128]{3,2,0,1:T(8,128)(2,1)S(1)} %get-tuple-element.165), channel_id=1, source_target_pairs={{0,8},{8,16},{16,24},{24,32},{32,40},{40,48},{48,56},{56,64},{64,7... | collective-permute-start | bytes 49160 | tf_op jit(solution)/shard_map/ppermute | solution.py:19
  75.9 9.0 %collective-permute-start.25 = (bf16[8,1,8,128]{3,2,0,1:T(8,128)(2,1)S(1)}, bf16[8,1,8,128]{3,2,0,1:T(8,128)(2,1)S(1)}, u32[]{:S(2)}, u32[]{:S(2)}) collective-permute-start(bf16[8,1,8,128]{3,2,0,1:T(8,128)(2,1)S(1)} %get-tuple-element.166), channel_id=1, source_target_pairs={{8,0},{16,8},{24,16},{32,24},{40,32},{48,40},{56,48},{64,56},{72,6... | collective-permute-start | bytes 49160 | tf_op jit(solution)/shard_map/ppermute | solution.py:22
  77.4 15.6 %collective-permute-start.10 = (bf16[8,10,1,128]{3,2,0,1:T(2,128)(2,1)S(1)}, bf16[8,10,1,128]{3,2,0,1:T(2,128)(2,1)S(1)}, u32[]{:S(2)}, u32[]{:S(2)}) collective-permute-start(bf16[8,10,1,128]{3,2,0,1:T(2,128)(2,1)S(1)} %get-tuple-element.141), channel_id=1, source_target_pairs={{0,1},{1,2},{2,3},{3,4},{4,5},{5,6},{6,7},{8,9},{9,10},{10,11},{11... | collective-permute-start | bytes 61448 | tf_op jit(solution)/shard_map/ppermute | solution.py:19
  83.0 10.0 %collective-permute-start.11 = (bf16[8,10,1,128]{3,2,0,1:T(2,128)(2,1)S(1)}, bf16[8,10,1,128]{3,2,0,1:T(2,128)(2,1)S(1)}, u32[]{:S(2)}, u32[]{:S(2)}) collective-permute-start(bf16[8,10,1,128]{3,2,0,1:T(2,128)(2,1)S(1)} %get-tuple-element.142), channel_id=1, source_target_pairs={{1,0},{2,1},{3,2},{4,3},{5,4},{6,5},{7,6},{9,8},{10,9},{11,10},{12... | collective-permute-start | bytes 61448 | tf_op jit(solution)/shard_map/ppermute | solution.py:22
  85.0 9.6 %collective-permute-start.26 = (bf16[8,10,1,128]{3,2,0,1:T(2,128)(2,1)S(1)}, bf16[8,10,1,128]{3,2,0,1:T(2,128)(2,1)S(1)}, u32[]{:S(2)}, u32[]{:S(2)}) collective-permute-start(bf16[8,10,1,128]{3,2,0,1:T(2,128)(2,1)S(1)} %get-tuple-element.149), channel_id=1, source_target_pairs={{0,1},{1,2},{2,3},{3,4},{4,5},{5,6},{6,7},{8,9},{9,10},{10,11},{11... | collective-permute-start | bytes 61448 | tf_op jit(solution)/shard_map/ppermute | solution.py:19
  98.6 15.3 %collective-permute-start.12 = (bf16[8,1,8,128]{3,2,0,1:T(8,128)(2,1)S(1)}, bf16[8,1,8,128]{3,2,0,1:T(8,128)(2,1)S(1)}, u32[]{:S(2)}, u32[]{:S(2)}) collective-permute-start(bf16[8,1,8,128]{3,2,0,1:T(8,128)(2,1)S(1)} %get-tuple-element.155), channel_id=1, source_target_pairs={{0,8},{8,16},{16,24},{24,32},{32,40},{40,48},{48,56},{56,64},{64,7... | collective-permute-start | bytes 49160 | tf_op jit(solution)/shard_map/ppermute | solution.py:19
  102.6 11.3 %collective-permute-start.13 = (bf16[8,1,8,128]{3,2,0,1:T(8,128)(2,1)S(1)}, bf16[8,1,8,128]{3,2,0,1:T(8,128)(2,1)S(1)}, u32[]{:S(2)}, u32[]{:S(2)}) collective-permute-start(bf16[8,1,8,128]{3,2,0,1:T(8,128)(2,1)S(1)} %get-tuple-element.156), channel_id=1, source_target_pairs={{8,0},{16,8},{24,16},{32,24},{40,32},{48,40},{56,48},{64,56},{72,6... | collective-permute-start | bytes 49160 | tf_op jit(solution)/shard_map/ppermute | solution.py:22
  104.1 16.5 %collective-permute-start.28 = (bf16[8,1,8,128]{3,2,0,1:T(8,128)(2,1)S(1)}, bf16[8,1,8,128]{3,2,0,1:T(8,128)(2,1)S(1)}, u32[]{:S(2)}, u32[]{:S(2)}) collective-permute-start(bf16[8,1,8,128]{3,2,0,1:T(8,128)(2,1)S(1)} %get-tuple-element.163), channel_id=1, source_target_pairs={{0,8},{8,16},{16,24},{24,32},{32,40},{40,48},{48,56},{56,64},{64,7... | collective-permute-start | bytes 49160 | tf_op jit(solution)/shard_map/ppermute | solution.py:19
  114.0 14.7 %collective-permute-start.14 = (bf16[8,10,1,128]{3,2,0,1:T(2,128)(2,1)S(1)}, bf16[8,10,1,128]{3,2,0,1:T(2,128)(2,1)S(1)}, u32[]{:S(2)}, u32[]{:S(2)}) collective-permute-start(bf16[8,10,1,128]{3,2,0,1:T(2,128)(2,1)S(1)} %get-tuple-element.139), channel_id=1, source_target_pairs={{0,1},{1,2},{2,3},{3,4},{4,5},{5,6},{6,7},{8,9},{9,10},{10,11},{11... | collective-permute-start | bytes 61448 | tf_op jit(solution)/shard_map/ppermute | solution.py:19
  118.7 10.0 %collective-permute-start.15 = (bf16[8,10,1,128]{3,2,0,1:T(2,128)(2,1)S(1)}, bf16[8,10,1,128]{3,2,0,1:T(2,128)(2,1)S(1)}, u32[]{:S(2)}, u32[]{:S(2)}) collective-permute-start(bf16[8,10,1,128]{3,2,0,1:T(2,128)(2,1)S(1)} %get-tuple-element.140), channel_id=1, source_target_pairs={{1,0},{2,1},{3,2},{4,3},{5,4},{6,5},{7,6},{9,8},{10,9},{11,10},{12... | collective-permute-start | bytes 61448 | tf_op jit(solution)/shard_map/ppermute | solution.py:22
  120.7 9.6 %collective-permute-start.30 = (bf16[8,10,1,128]{3,2,0,1:T(2,128)(2,1)S(1)}, bf16[8,10,1,128]{3,2,0,1:T(2,128)(2,1)S(1)}, u32[]{:S(2)}, u32[]{:S(2)}) collective-permute-start(bf16[8,10,1,128]{3,2,0,1:T(2,128)(2,1)S(1)} %get-tuple-element.147), channel_id=1, source_target_pairs={{0,1},{1,2},{2,3},{3,4},{4,5},{5,6},{6,7},{8,9},{9,10},{10,11},{11... | collective-permute-start | bytes 61448 | tf_op jit(solution)/shard_map/ppermute | solution.py:19
  134.3 15.5 %collective-permute-start.16 = (bf16[8,1,8,128]{3,2,0,1:T(8,128)(2,1)S(1)}, bf16[8,1,8,128]{3,2,0,1:T(8,128)(2,1)S(1)}, u32[]{:S(2)}, u32[]{:S(2)}) collective-permute-start(bf16[8,1,8,128]{3,2,0,1:T(8,128)(2,1)S(1)} %get-tuple-element.153), channel_id=1, source_target_pairs={{0,8},{8,16},{16,24},{24,32},{32,40},{40,48},{48,56},{56,64},{64,7... | collective-permute-start | bytes 49160 | tf_op jit(solution)/shard_map/ppermute | solution.py:19
  138.9 10.9 %collective-permute-start.17 = (bf16[8,1,8,128]{3,2,0,1:T(8,128)(2,1)S(1)}, bf16[8,1,8,128]{3,2,0,1:T(8,128)(2,1)S(1)}, u32[]{:S(2)}, u32[]{:S(2)}) collective-permute-start(bf16[8,1,8,128]{3,2,0,1:T(8,128)(2,1)S(1)} %get-tuple-element.154), channel_id=1, source_target_pairs={{8,0},{16,8},{24,16},{32,24},{40,32},{48,40},{56,48},{64,56},{72,6... | collective-permute-start | bytes 49160 | tf_op jit(solution)/shard_map/ppermute | solution.py:22
  140.4 15.5 %collective-permute-start.32 = (bf16[8,1,8,128]{3,2,0,1:T(8,128)(2,1)S(1)}, bf16[8,1,8,128]{3,2,0,1:T(8,128)(2,1)S(1)}, u32[]{:S(2)}, u32[]{:S(2)}) collective-permute-start(bf16[8,1,8,128]{3,2,0,1:T(8,128)(2,1)S(1)} %get-tuple-element.161), channel_id=1, source_target_pairs={{0,8},{8,16},{16,24},{24,32},{32,40},{40,48},{48,56},{56,64},{64,7... | collective-permute-start | bytes 49160 | tf_op jit(solution)/shard_map/ppermute | solution.py:19
  149.9 14.0 %collective-permute-start.18 = (bf16[8,10,1,128]{3,2,0,1:T(2,128)(2,1)S(1)}, bf16[8,10,1,128]{3,2,0,1:T(2,128)(2,1)S(1)}, u32[]{:S(2)}, u32[]{:S(2)}) collective-permute-start(bf16[8,10,1,128]{3,2,0,1:T(2,128)(2,1)S(1)} %get-tuple-element.137), channel_id=1, source_target_pairs={{0,1},{1,2},{2,3},{3,4},{4,5},{5,6},{6,7},{8,9},{9,10},{10,11},{11... | collective-permute-start | bytes 61448 | tf_op jit(solution)/shard_map/ppermute | solution.py:19
  153.9 10.0 %collective-permute-start.19 = (bf16[8,10,1,128]{3,2,0,1:T(2,128)(2,1)S(1)}, bf16[8,10,1,128]{3,2,0,1:T(2,128)(2,1)S(1)}, u32[]{:S(2)}, u32[]{:S(2)}) collective-permute-start(bf16[8,10,1,128]{3,2,0,1:T(2,128)(2,1)S(1)} %get-tuple-element.138), channel_id=1, source_target_pairs={{1,0},{2,1},{3,2},{4,3},{5,4},{6,5},{7,6},{9,8},{10,9},{11,10},{12... | collective-permute-start | bytes 61448 | tf_op jit(solution)/shard_map/ppermute | solution.py:22
  155.9 17.8 %collective-permute-start.34 = (bf16[8,10,1,128]{3,2,0,1:T(2,128)(2,1)S(1)}, bf16[8,10,1,128]{3,2,0,1:T(2,128)(2,1)S(1)}, u32[]{:S(2)}, u32[]{:S(2)}) collective-permute-start(bf16[8,10,1,128]{3,2,0,1:T(2,128)(2,1)S(1)} %get-tuple-element.145), channel_id=1, source_target_pairs={{0,1},{1,2},{2,3},{3,4},{4,5},{5,6},{6,7},{8,9},{9,10},{10,11},{11... | collective-permute-start | bytes 61448 | tf_op jit(solution)/shard_map/ppermute | solution.py:19
  162.0 11.7 %collective-permute-start.35 = (bf16[8,10,1,128]{3,2,0,1:T(2,128)(2,1)S(1)}, bf16[8,10,1,128]{3,2,0,1:T(2,128)(2,1)S(1)}, u32[]{:S(2)}, u32[]{:S(2)}) collective-permute-start(bf16[8,10,1,128]{3,2,0,1:T(2,128)(2,1)S(1)} %get-tuple-element.146), channel_id=1, source_target_pairs={{1,0},{2,1},{3,2},{4,3},{5,4},{6,5},{7,6},{9,8},{10,9},{11,10},{12... | collective-permute-start | bytes 61448 | tf_op jit(solution)/shard_map/ppermute | solution.py:22
  166.1 15.6 %all-to-all-start = ((bf16[32,8,8,128]{3,2,0,1:T(8,128)(2,1)}), bf16[32,8,8,128]{3,2,0,1:T(8,128)(2,1)S(1)}, u32[]{:S(2)}, u32[]{:S(2)}) async-start(bf16[32,8,8,128]{3,2,0,1:T(8,128)(2,1)} %pad_maximum_fusion.1), calls=%async_computation | async-start | bytes 1048576 | tf_op jit(solution)/shard_map/all_to_all | solution.py:165
  181.7 14.4 %all-to-all-start.1 = ((bf16[32,8,8,128]{3,2,0,1:T(8,128)(2,1)}), bf16[32,8,8,128]{3,2,0,1:T(8,128)(2,1)S(1)}, u32[]{:S(2)}, u32[]{:S(2)}) async-start(bf16[32,8,8,128]{3,2,0,1:T(8,128)(2,1)} %pad_maximum_fusion.2), calls=%async_computation.1 | async-start | bytes 1048576 | tf_op jit(solution)/shard_map/all_to_all | solution.py:165
  187.7 100.1 %all-reduce.24.cloned.1.call-start = ((), (), s32[]{:S(2)}) async-start(), calls=%async_computation.2 | async-start | bytes 983040 | tf_op jit(solution)/shard_map/psum | solution.py:183
  199.9 374.8 %all-reduce.26.cloned.1.call-start = ((), (), s32[]{:S(2)}) async-start(), calls=%async_computation.3 | async-start | bytes 983040 | tf_op jit(solution)/shard_map/psum | solution.py:183
  (18 other events, 269.4 us)
Sparse Core Ops, SparseCore 0:
  200.0 87.6 all-reduce.23
  290.4 284.3 all-reduce.25
